TPU v7x, 128 devices: a whole 4x4x4 slice. The times are simulated.
128 devices in a mesh: dp: 64 (over y, z_hi, x, core), mod: 2 (over z_lo).
Axes of the slice: x: 4, y: 4, z: 4 (z_hi: 2, z_lo: 2; z = z_hi * 2 + z_lo), core: 2. Of those that a mesh axis runs over, the one named last changes fastest.
Arguments:
- tokens: bfloat16 [256, 256, 1024], P(('dp', 'mod')), may hold values from -6 to 6
- condition: bfloat16 [256, 1024], P(('dp', 'mod')), may hold values from -6 to 6
- occupied: int32 [256], P(('dp', 'mod')), may hold values from 0 to 1, as said below
- modulation_weight: bfloat16 [1024, 6144], P(None, 'mod'), may hold values from -0.1875 to 0.1875
- modulation_bias: float32 [6, 1024], P('mod'), may hold values from -3 to 3
- input_weight: bfloat16 [1024, 3072], replicated, may hold values from -0.1875 to 0.1875
- query_bias: float32 [1024], replicated, may hold values from -3 to 3
- value_bias: float32 [1024], replicated, may hold values from -3 to 3
- output_weight: bfloat16 [1024, 1024], replicated, may hold values from -1.5 to 1.5
- output_bias: float32 [1024], replicated, may hold values from -3 to 3
- expand_weight: bfloat16 [1024, 4096], replicated, may hold values from -0.1875 to 0.1875
- expand_bias: float32 [4096], replicated, may hold values from -3 to 3
- contract_weight: bfloat16 [4096, 1024], replicated, may hold values from -0.1875 to 0.1875
- contract_bias: float32 [1024], replicated, may hold values from -3 to 3
- cotangent: bfloat16 [256, 256, 1024], P(('dp', 'mod')), may hold values from -6 to 6
Outputs:
- layer_out: float32 [256, 256, 1024], P(('dp', 'mod'))
- tokens_grad: float32 [256, 256, 1024], P(('dp', 'mod'))
- condition_grad: float32 [256, 1024], P(('dp', 'mod'))
- modulation_weight_grad: float32 [1024, 6144], P('dp', 'mod')
- modulation_bias_grad: float32 [6, 1024], P('mod', 'dp')
- input_weight_grad: float32 [1024, 3072], P(('dp', 'mod'))
- query_bias_grad: float32 [1024], P(('dp', 'mod'))
- value_bias_grad: float32 [1024], P(('dp', 'mod'))
- output_weight_grad: float32 [1024, 1024], P(('dp', 'mod'))
- output_bias_grad: float32 [1024], P(('dp', 'mod'))
- expand_weight_grad: float32 [1024, 4096], P(('dp', 'mod'))
- expand_bias_grad: float32 [4096], P(('dp', 'mod'))
- contract_weight_grad: float32 [4096, 1024], P(('dp', 'mod'))
- contract_bias_grad: float32 [1024], P(('dp', 'mod'))
Inputs may be any that keep to these rules, and one draw needn't show every extreme that they name: Slots come in aligned groups of 2 held by one device; the images of a group with occupied = 1 are its first 1 to 2 slots, every group has one, and some group has all 2.
All inputs are finite; a program needn't handle non-finite values.
Results may differ from a plain program's by a relative error of at most 0.017.
The roundings to bfloat16 on the way count: a program that leaves them out, or rounds other values in their place, can miss the bound.
Values may be sent and summed in bfloat16 or wider, within the bound.
No kernel may reach another device: no remote copies, remote signals or barrier semaphores. Data moves between devices by JAX's collectives and lax.ppermute only.
A program may use at most 256 MiB of HBM per device.

v0:
```python
import jax
import jax.numpy as jnp
import numpy as np
from jax import lax
from jax.sharding import Mesh
from jax.sharding import PartitionSpec as P

HEAD_DIM = 64


EPS = 1e-06
GELU_C = 0.7978845608028654

AXES = ("y", "zh", "x", "c", "zl")
DP = ("y", "zh", "x", "c")
STAGES = ("c", "x", "y", "zh", "zl")


def matmul(left, right):
    return jnp.dot(left, right, preferred_element_type=jnp.float32)


def left_trans(left, right):
    return lax.dot_general(
        left, right, (((0,), (0,)), ((), ())), preferred_element_type=jnp.float32
    )


def right_trans(left, right):
    return lax.dot_general(
        left, right, (((1,), (1,)), ((), ())), preferred_element_type=jnp.float32
    )


def normalize(values):
    centre = values - jnp.mean(values, axis=-1, keepdims=True)
    inverse = lax.rsqrt(jnp.mean(centre * centre, axis=-1, keepdims=True) + EPS)
    return (centre * inverse, inverse)


def norm_back(grad, normed, inverse):
    return inverse * (
        grad
        - jnp.mean(grad, axis=-1, keepdims=True)
        - normed * jnp.mean(grad * normed, axis=-1, keepdims=True)
    )


def stage_order(values, sizes, inner):
    lead = values.shape[:-1]
    shape = [sizes[a] for a in AXES]
    values = values.reshape(*lead, *shape, inner)
    n = len(lead)
    order = list(range(n)) + [n + AXES.index(a) for a in STAGES] + [n + len(AXES)]
    return jnp.transpose(values, order).reshape(*lead, -1)


def reduce_stages(packed):
    for a in STAGES:
        packed = lax.psum_scatter(packed, a, scatter_dimension=0, tiled=True)
    return packed.astype(jnp.float32)


def bias_columns(columns, rows):
    block = jnp.stack(columns, axis=1)
    return jnp.pad(block, ((0, 0), (0, 128 - block.shape[1]))).astype(jnp.bfloat16)


def gather_dp(values):
    for a in ("c", "x", "zh", "y"):
        values = lax.all_gather(values, a, axis=0, tiled=True)
    return values


def per_device(
    sizes,
    tokens,
    condition,
    occupied,
    modulation_weight,
    modulation_bias,
    input_weight,
    query_bias,
    value_bias,
    output_weight,
    output_bias,
    expand_weight,
    expand_bias,
    contract_weight,
    contract_bias,
    cotangent,
):
    images, rows, width = tokens.shape
    heads = width // HEAD_DIM
    flat = images * rows
    factor = HEAD_DIM ** (-0.5)
    cond_full = condition.astype(jnp.float32)
    sigmoid = jax.nn.sigmoid(cond_full)
    silu_b = (cond_full * sigmoid).astype(jnp.bfloat16)
    silu_pair = lax.all_gather(silu_b, "zl", axis=0, tiled=True)
    mod_cols = matmul(silu_pair, modulation_weight) + modulation_bias.reshape(1, -1)
    modulation = lax.all_to_all(mod_cols, "zl", split_axis=0, concat_axis=1, tiled=True).reshape(
        images, 6, 1, width
    )
    shift_a = modulation[:, 0]
    scale_a = modulation[:, 1]
    gate_a = modulation[:, 2]
    shift_b = modulation[:, 3]
    scale_b = modulation[:, 4]
    gate_b = modulation[:, 5]
    inputs = tokens.astype(jnp.float32)
    normed_a, inverse_a = normalize(inputs)
    mod_a = (normed_a * (1.0 + scale_a) + shift_a).astype(jnp.bfloat16).reshape(flat, width)
    qkv_bias = jnp.concatenate([query_bias, jnp.zeros_like(query_bias), value_bias])
    projected = (matmul(mod_a, input_weight) + qkv_bias).astype(jnp.bfloat16)
    queries = projected[:, :width].reshape(images, rows, heads, HEAD_DIM)
    keys_all = projected[:, width : 2 * width].reshape(images, rows, heads, HEAD_DIM)
    values_all = projected[:, 2 * width :].reshape(images, rows, heads, HEAD_DIM)
    scores = (
        jnp.einsum("bqhe,bkhe->bhqk", queries, keys_all, preferred_element_type=jnp.float32)
        * factor
    )
    highest = jnp.max(scores, axis=-1, keepdims=True)
    weights = jnp.exp(scores - highest)
    probs = weights / jnp.sum(weights, axis=-1, keepdims=True)
    probs_b = probs.astype(jnp.bfloat16)
    attended = jnp.einsum(
        "bhqk,bkhe->bqhe", probs_b, values_all, preferred_element_type=jnp.float32
    )
    attended_b = attended.reshape(flat, width).astype(jnp.bfloat16)
    branch_a = (matmul(attended_b, output_weight) + output_bias).reshape(images, rows, width)
    middle = inputs + gate_a * branch_a
    normed_b, inverse_b = normalize(middle)
    mod_b = (normed_b * (1.0 + scale_b) + shift_b).astype(jnp.bfloat16).reshape(flat, width)
    expanded = matmul(mod_b, expand_weight) + expand_bias
    tanh_part = jnp.tanh(GELU_C * (expanded + 0.044715 * expanded * expanded * expanded))
    activated_b = (0.5 * expanded * (1.0 + tanh_part)).astype(jnp.bfloat16)
    branch_b = (matmul(activated_b, contract_weight) + contract_bias).reshape(images, rows, width)
    alive = occupied.astype(jnp.float32)[:, None, None]
    layer_out = (middle + gate_b * branch_b) * alive
    grad_out = cotangent.astype(jnp.float32) * alive
    grad_gate_b = jnp.sum(grad_out * branch_b, axis=1)
    grad_branch_b = (grad_out * gate_b).astype(jnp.bfloat16).reshape(flat, width)
    blocks = 1
    for a in AXES:
        blocks *= sizes[a]
    ff = activated_b.shape[1]
    split = ff // width
    act_perm = stage_order(
        activated_b.reshape(flat, blocks, split, width // blocks)
        .transpose(0, 2, 1, 3)
        .reshape(flat, split, width),
        sizes,
        width // blocks,
    )
    contract_parts = [
        left_trans(act_perm[:, q], grad_branch_b).astype(jnp.bfloat16) for q in range(split)
    ]
    contract_bias_grad = stage_order(
        jnp.sum(grad_branch_b.astype(jnp.float32), axis=0), sizes, width // blocks
    )
    grad_act = right_trans(grad_branch_b, contract_weight)
    slope = 0.5 * (1.0 + tanh_part) + 0.5 * expanded * (1.0 - tanh_part * tanh_part) * GELU_C * (
        1.0 + 3.0 * 0.044715 * expanded * expanded
    )
    grad_exp_b = (grad_act * slope).astype(jnp.bfloat16)
    expand_grad = left_trans(stage_order(mod_b, sizes, width // blocks), grad_exp_b).astype(jnp.bfloat16)
    expand_bias_grad = stage_order(
        jnp.sum(grad_exp_b.astype(jnp.float32), axis=0)
        .reshape(blocks, split, width // blocks)
        .transpose(1, 0, 2)
        .reshape(split, width),
        sizes,
        width // blocks,
    )
    chain_a = reduce_stages(
        jnp.concatenate(
            [expand_grad]
            + contract_parts
            + [bias_columns([contract_bias_grad] + [expand_bias_grad[q] for q in range(split)], width)],
            axis=1,
        )
    )
    grad_mod_b = right_trans(grad_exp_b, expand_weight).reshape(images, rows, width)
    grad_shift_b = jnp.sum(grad_mod_b, axis=1)
    grad_scale_b = jnp.sum(grad_mod_b * normed_b, axis=1)
    grad_middle = grad_out + norm_back(grad_mod_b * (1.0 + scale_b), normed_b, inverse_b)
    grad_gate_a = jnp.sum(grad_middle * branch_a, axis=1)
    grad_branch_a = (grad_middle * gate_a).astype(jnp.bfloat16).reshape(flat, width)
    output_grad = left_trans(stage_order(attended_b, sizes, width // blocks), grad_branch_a).astype(
        jnp.bfloat16
    )
    output_bias_grad = stage_order(
        jnp.sum(grad_branch_a.astype(jnp.float32), axis=0), sizes, width // blocks
    )
    grad_att_b = (
        right_trans(grad_branch_a, output_weight)
        .astype(jnp.bfloat16)
        .reshape(images, rows, heads, HEAD_DIM)
    )
    grad_probs = jnp.einsum(
        "bqhe,bkhe->bhqk", grad_att_b, values_all, preferred_element_type=jnp.float32
    )
    grad_values = jnp.einsum(
        "bhqk,bqhe->bkhe", probs_b, grad_att_b, preferred_element_type=jnp.float32
    )
    inner = jnp.sum(grad_probs * probs, axis=-1, keepdims=True)
    grad_scores_b = (probs * (grad_probs - inner)).astype(jnp.bfloat16)
    grad_queries = (
        jnp.einsum("bhqk,bkhe->bqhe", grad_scores_b, keys_all, preferred_element_type=jnp.float32)
        * factor
    )
    grad_keys = (
        jnp.einsum("bhqk,bqhe->bkhe", grad_scores_b, queries, preferred_element_type=jnp.float32)
        * factor
    )
    grad_proj_b = jnp.concatenate(
        [
            grad_queries.reshape(flat, width),
            grad_keys.reshape(flat, width),
            grad_values.reshape(flat, width),
        ],
        axis=1,
    ).astype(jnp.bfloat16)
    input_grad = left_trans(stage_order(mod_a, sizes, width // blocks), grad_proj_b).astype(jnp.bfloat16)
    bias_sums = jnp.sum(grad_proj_b.astype(jnp.float32), axis=0)
    query_bias_grad = stage_order(bias_sums[:width], sizes, width // blocks)
    value_bias_grad = stage_order(bias_sums[2 * width :], sizes, width // blocks)
    chain_b = reduce_stages(
        jnp.concatenate(
            [
                input_grad,
                output_grad,
                bias_columns([query_bias_grad, value_bias_grad, output_bias_grad], width),
            ],
            axis=1,
        )
    )
    grad_mod_a = right_trans(grad_proj_b, input_weight).reshape(images, rows, width)
    grad_shift_a = jnp.sum(grad_mod_a, axis=1)
    grad_scale_a = jnp.sum(grad_mod_a * normed_a, axis=1)
    tokens_grad = grad_middle + norm_back(grad_mod_a * (1.0 + scale_a), normed_a, inverse_a)
    modulation_terms = jnp.stack(
        [grad_shift_a, grad_scale_a, grad_gate_a, grad_shift_b, grad_scale_b, grad_gate_b], axis=1
    ).reshape(images, 6 * width)
    modulation_own = modulation_terms.astype(jnp.bfloat16)
    modulation_cols = lax.all_to_all(modulation_own, "zl", split_axis=1, concat_axis=0, tiled=True)
    silu_terms = right_trans(modulation_cols, modulation_weight)
    silu_sums = lax.psum_scatter(silu_terms, "zl", scatter_dimension=0, tiled=True)
    condition_grad = silu_sums * sigmoid * (1.0 + cond_full * (1.0 - sigmoid))
    factors = gather_dp(jnp.concatenate([silu_pair, modulation_cols], axis=1))
    silu_all = factors[:, :width]
    mod_all = factors[:, width:]
    dp_index = lax.axis_index(DP)
    dp_count = factors.shape[0] // silu_pair.shape[0]
    row_block = width // dp_count
    silu_rows = lax.dynamic_slice_in_dim(silu_all, dp_index * row_block, row_block, axis=1)
    modulation_weight_grad = left_trans(silu_rows, mod_all)
    bias_all = jnp.sum(mod_all.astype(jnp.float32), axis=0).reshape(-1, width)
    modulation_bias_grad = lax.dynamic_slice_in_dim(bias_all, dp_index * row_block, row_block, axis=1)
    three = input_weight.shape[1]
    fw = expand_weight.shape[1]
    input_weight_grad = chain_b[:, :three]
    output_weight_grad = chain_b[:, three : three + width]
    qb_grad = chain_b[:, three + width]
    vb_grad = chain_b[:, three + width + 1]
    ob_grad = chain_b[:, three + width + 2]
    expand_weight_grad = chain_a[:, :fw]
    contract_weight_grad = chain_a[:, fw : fw + split * width].reshape(-1, split, width)
    contract_weight_grad = contract_weight_grad.transpose(1, 0, 2).reshape(-1, width)
    cb_grad = chain_a[:, fw + split * width]
    eb_grad = chain_a[:, fw + split * width + 1 : fw + split * width + 1 + split].T.reshape(-1)
    summed = (
        input_weight_grad,
        qb_grad,
        vb_grad,
        output_weight_grad,
        ob_grad,
        expand_weight_grad,
        eb_grad,
        contract_weight_grad,
        cb_grad,
    )
    return (
        layer_out,
        tokens_grad,
        condition_grad,
        modulation_weight_grad,
        modulation_bias_grad,
        *summed,
    )


def solution(mesh):
    dp_size, mod_size = mesh.devices.shape
    rest = dp_size // 4
    side = int(round(rest ** 0.5))
    shape = (side, 2, rest // side, 2, mod_size)
    sizes = dict(zip(AXES, shape))
    physical = Mesh(np.asarray(mesh.devices).reshape(shape), AXES)
    ALL = AXES
    placed = (
        P(ALL, None, None),
        P(ALL, None),
        P(ALL),
        P(None, "zl"),
        P("zl", None),
        P(),
        P(),
        P(),
        P(),
        P(),
        P(),
        P(),
        P(),
        P(),
        P(ALL, None, None),
    )
    import functools

    return jax.shard_map(
        functools.partial(per_device, sizes),
        mesh=physical,
        in_specs=placed,
        out_specs=(
            P(ALL, None, None),
            P(ALL, None, None),
            P(ALL, None),
            P(DP, "zl"),
            P("zl", DP),
            P(ALL, None),
            P(ALL),
            P(ALL),
            P(ALL, None),
            P(ALL),
            P(ALL, None),
            P(ALL),
            P(ALL, None),
            P(ALL),
        ),
        check_vma=False,
    )
```

profile of v0, /device:TPU:24, one launch (start us, length us, event | category | flops | bytes accessed | tf_op | source)
XLA Modules:
  0.0 564.6 jit_solution(4670281731506859715)
XLA Ops:
  8.1 4.5 all-gather
  13.3 3.7 convolution_add_fusion
  17.7 3.3 all-to-all-start
  21.8 3.2 all-to-all-done
  25.6 6.8 %add_convert_fusion = bf16[512,3072]{1,0:T(8,128)(2,1)S(1)} fusion(bf16[512,1024]{1,0:T(8,128)(2,1)S(1)} %bitcast.196, bf16[1024,3072]{1,0:T(8,128)(2,1)} %param.20, f32[3072]{0:T(1024)S(1)} %pad_maximum_fusion), kind=kOutput, calls=%fused_computation.20 | convolution fusion | flops 3224371200 | bytes 10498048 | tf_op jit(solution)/shard_map/dot_general | solution.py:20
  34.2 4.0 reshape.290
  38.2 3.5 copy.165
  41.8 4.0 reshape.291
  45.8 3.6 copy.163
  49.3 4.0 reshape.292
  53.3 3.7 copy.164
  57.1 7.6 %fusion.72 = (f32[2,16,256]{2,1,0:T(8,128)S(1)}, f32[2,16,256,256]{2,3,1,0:T(8,128)}) fusion(bf16[2,256,16,64]{1,3,2,0:T(8,128)(2,1)} %copy.163, bf16[2,256,16,64]{1,3,2,0:T(8,128)(2,1)} %copy.164), kind=kOutput, calls=%fused_computation.147 | convolution fusion | flops 274727168 | bytes 10518528 | tf_op jit(solution)/shard_map/sub | solution.py:124
  64.7 4.6 fusion.46
  74.0 2.9 slice-done.3
  77.0 8.5 %multiply_convert_fusion.1 = (bf16[512,4096]{1,0:T(8,128)(2,1)S(1)}, f32[512,4096]{1,0:T(8,128)}) fusion(f32[4096]{0:T(1024)S(1)} %copy-done.39, bf16[512,1024]{1,0:T(8,128)(2,1)S(1)} %bitcast.195, bf16[1024,4096]{1,0:T(8,128)(2,1)S(1)} %bitcast.227), kind=kOutput, calls=%fused_computation.16 | convolution fusion | flops 4315938816 | bytes 22036480 | tf_op jit(solution)/shard_map/dot_general | solution.py:20
  85.9 16.7 %fusion.73 = (bf16[4096]{0:T(1024)(128)(2,1)S(1)}, bf16[512,4096]{1,0:T(8,128)(2,1)}) fusion(f32[512,4096]{1,0:T(8,128)} %get-tuple-element.56, f32[4096]{0:T(1024)S(1)} %copy-done.39, bf16[512,1024]{1,0:T(8,128)(2,1)S(1)} %bitcast.206, bf16[4096,1024]{1,0:T(8,128)(2,1)} %param.27), kind=kOutput, calls=%fused_computation.148 | convolution fusion | flops 4339003392 | bytes 22044672 | tf_op jit(solution)/shard_map/dot_general | solution.py:30
  102.7 6.5 %fusion.29 = (f32[512]{0:T(512)S(1)}, f32[512,1024]{1,0:T(8,128)S(1)}) fusion(f32[2,1024]{1,0:T(2,128)S(1)} %get-tuple-element.46, bf16[512,4096]{1,0:T(8,128)(2,1)} %get-tuple-element.64, bf16[1024,4096]{1,0:T(8,128)(2,1)S(1)} %bitcast.227), kind=kOutput, calls=%fused_computation.47 | convolution fusion | flops 4296015360 | bytes 14690304 | tf_op jit(solution)/shard_map/dot_general | solution.py:30
  109.2 7.6 %convolution_add_fusion.2 = f32[512,1024]{1,0:T(8,128)S(1)} fusion(bf16[512,4096]{1,0:T(8,128)(2,1)S(1)} %get-tuple-element.55, bf16[4096,1024]{1,0:T(8,128)(2,1)} %param.27, f32[1024]{0:T(1024)S(1)} %copy-done.40), kind=kOutput, calls=%fused_computation.74 | convolution fusion | flops 4295491584 | bytes 14684160 | tf_op jit(solution)/shard_map/dot_general | solution.py:20
  116.9 2.8 fusion.30
  119.7 4.9 fusion.66
  127.9 3.1 reshape.293
  133.5 5.6 multiply_reduce_fusion
  139.1 4.5 multiply_convert_fusion
  169.3 3.8 convolution_convert_fusion.1
  173.9 5.7 %convolution_convert_fusion = bf16[1024,3072]{1,0:T(8,128)(2,1)S(1)} fusion(bf16[512,1024]{0,1:T(8,128)(2,1)S(1)} %bitcast.213, bf16[512,3072]{0,1:T(8,128)(2,1)} %constant_dynamic-update-slice_fusion), kind=kOutput, calls=%fused_computation.21 | convolution fusion | flops 3224371200 | bytes 10485760 | tf_op jit(solution)/shard_map/dot_general | solution.py:24
  179.6 3.7 fusion.2
  185.7 6.5 %copy.193 = bf16[512,4096]{0,1:T(8,128)(2,1)} copy(bf16[512,4096]{1,0:T(8,128)(2,1)} %copy-done.11) | data formatting | bytes 8388608 | tf_op jit(solution)/shard_map/convert_element_type | solution.py:137
  193.0 6.0 %copy.194 = bf16[512,4,4,2,4,2,2,8]{0,7,6,3,2,4,5,1:T(8,128)(2,1)} copy(bf16[512,4,4,2,4,2,2,8]{0,7,1,6,5,4,3,2:T(8,128)(2,1)} %bitcast.186) | data formatting | bytes 8388608 | tf_op jit(solution)/shard_map/reshape;reshape | solution.py:52
  200.4 10.1 %convert_dynamic-update-slice_fusion = bf16[1024,8320]{1,0:T(8,128)(2,1)} fusion(bf16[512,1024]{0,1:T(8,128)(2,1)S(1)} %bitcast.211, bf16[512,4096]{1,0:T(8,128)(2,1)} %get-tuple-element.64), kind=kOutput, calls=%fused_computation.13 | convolution fusion | flops 4299161600 | bytes 13631488 | tf_op jit(solution)/shard_map/dot_general | solution.py:24
  210.4 2.7 convert_dynamic-update-slice_fusion.4
  213.1 2.7 convert_dynamic-update-slice_fusion.3
  215.8 2.7 convert_dynamic-update-slice_fusion.2
  218.5 2.7 convert_dynamic-update-slice_fusion.1
  222.8 30.3 %reduce-scatter.17.cloned.1.call-done = bf16[512,8320]{1,0:T(8,128)(2,1)} async-done(((bf16[1024,8320]{1,0:T(8,128)(2,1)}), bf16[512,8320]{1,0:T(8,128)(2,1)}) %reduce-scatter.17.cloned.1.call-update) | async-done | bytes 8519696 | tf_op jit(solution)/shard_map/reduce_scatter | solution.py:60
  253.2 51.6 %reduce-scatter.11.cloned.1.call-done = bf16[128,4224]{1,0:T(8,128)(2,1)} async-done(((bf16[512,4224]{1,0:T(8,128)(2,1)}), bf16[128,4224]{1,0:T(8,128)(2,1)}) %reduce-scatter.11.cloned.1.call-update) | async-done | bytes 1081360 | tf_op jit(solution)/shard_map/reduce_scatter | solution.py:60
  304.8 83.7 %reduce-scatter.19.cloned.1.call-done = bf16[128,8320]{1,0:T(8,128)(2,1)} async-done(((bf16[512,8320]{1,0:T(8,128)(2,1)}), bf16[128,8320]{1,0:T(8,128)(2,1)}) %reduce-scatter.19.cloned.1.call-update) | async-done | bytes 2129936 | tf_op jit(solution)/shard_map/reduce_scatter | solution.py:60
  388.9 8.5 %fusion.28 = (f32[512]{0:T(512)S(1)}, f32[512,1024]{1,0:T(8,128)}) fusion(f32[2,1024]{1,0:T(2,128)S(1)} %copy-done.28, bf16[512,3072]{0,1:T(8,128)(2,1)} %constant_dynamic-update-slice_fusion, bf16[1024,3072]{1,0:T(8,128)(2,1)} %param.20), kind=kOutput, calls=%fused_computation.44 | convolution fusion | flops 3222273536 | bytes 11544576 | tf_op jit(solution)/shard_map/dot_general | solution.py:30
  397.4 3.4 fusion.26
  401.1 3.9 multiply_reduce_fusion.3
  405.0 7.2 %reduce-scatter.13.cloned.1.call-done = bf16[32,4224]{1,0:T(8,128)(2,1)} async-done(((bf16[128,4224]{1,0:T(8,128)(2,1)}), bf16[32,4224]{1,0:T(8,128)(2,1)}) %reduce-scatter.13.cloned.1.call-update) | async-done | bytes 270352 | tf_op jit(solution)/shard_map/reduce_scatter | solution.py:60
  412.3 32.0 %reduce-scatter.21.cloned.1.call-done = bf16[32,8320]{1,0:T(8,128)(2,1)} async-done(((bf16[128,8320]{1,0:T(8,128)(2,1)}), bf16[32,8320]{1,0:T(8,128)(2,1)}) %reduce-scatter.21.cloned.1.call-update) | async-done | bytes 532496 | tf_op jit(solution)/shard_map/reduce_scatter | solution.py:60
  444.4 6.5 %all_to_all.32 = bf16[2,2,3072]{2,0,1:T(2,128)(2,1)S(1)} all-to-all(bf16[2,2,3072]{2,0,1:T(2,128)(2,1)S(1)} %bitcast.225), channel_id=1, replica_groups=mesh['y'=4,'zh'=2,'x'=4,'c'=2,'zl'=2] {'zl'}, dimensions={1} | all-to-all | bytes 49152 | tf_op jit(solution)/shard_map/all_to_all | solution.py:247
  452.9 12.6 %all_gather.17 = bf16[32,4096]{1,0:T(8,128)(2,1)S(1)} all-gather(bf16[8,4096]{1,0:T(8,128)(2,1)S(1)} %reshape.286), channel_id=1, replica_groups=mesh['y'=4,'zh'=2,'x'=4,'c'=2,'zl'=2] {'x'}, dimensions={0}, use_global_device_ids=true | all-gather | bytes 327680 | tf_op jit(solution)/shard_map/all_gather | solution.py:71
  465.5 8.6 %all_gather.18 = bf16[64,4096]{1,0:T(8,128)(2,1)} all-gather(bf16[32,4096]{1,0:T(8,128)(2,1)S(1)} %all_gather.17), channel_id=1, replica_groups=mesh['y'=4,'zh'=2,'x'=4,'c'=2,'zl'=2] {'zh'}, dimensions={0}, use_global_device_ids=true | all-gather | bytes 786432 | tf_op jit(solution)/shard_map/all_gather | solution.py:71
  476.1 4.7 fusion.74
  480.7 6.7 %all-reduce.2 = f32[4,1024]{1,0:T(4,128)S(1)} all-reduce(f32[4,1024]{1,0:T(4,128)S(1)} %fusion.74), channel_id=2, replica_groups=mesh['y'=4,'zh'=2,'x'=4,'c'=2,'zl'=2] {'zl'}, use_global_device_ids=true, to_apply=%region_17.18.clone | all-reduce | flops 4096 | bytes 32768
  488.1 26.7 %all-gather.4.cloned.1.call-done = bf16[256,4096]{1,0:T(8,128)(2,1)} async-done(((bf16[64,4096]{1,0:T(8,128)(2,1)}), bf16[256,4096]{1,0:T(8,128)(2,1)}) %all-gather.4.cloned.1.call-update) | async-done | bytes 2097168 | tf_op jit(solution)/shard_map/all_gather | solution.py:71
  520.7 31.2 %all-reduce.8.cloned.1.call-done = (bf16[16,4224]{1,0:T(8,128)(2,1)}, bf16[16,8320]{1,0:T(8,128)(2,1)}) async-done(((bf16[16,4224]{1,0:T(8,128)(2,1)}, bf16[16,8320]{1,0:T(8,128)(2,1)}), (bf16[16,4224]{1,0:T(8,128)(2,1)}, bf16[16,8320]{1,0:T(8,128)(2,1)})) %all-reduce.8.cloned.1.call-update) | async-done | bytes 401424
  (225 shorter events, 63.9 us)
Async XLA Ops:
  7.2 64.3 %copy-start = (bf16[1024,1024]{1,0:T(8,128)(2,1)S(1)}, bf16[1024,1024]{1,0:T(8,128)(2,1)}, u32[]{:S(2)}) copy-start(bf16[1024,1024]{1,0:T(8,128)(2,1)} %param.23) | copy-start | bytes 6291460
  7.2 13.9 %copy-start.3 = (bf16[2,256,1024]{2,1,0:T(8,128)(2,1)S(1)}, bf16[2,256,1024]{2,1,0:T(8,128)(2,1)}, u32[]{:S(2)}) copy-start(bf16[2,256,1024]{2,1,0:T(8,128)(2,1)} %param.15) | copy-start | bytes 3145732
  12.6 9.1 %copy-start.29 = (bf16[4,1024]{1,0:T(4,128)(2,1)}, bf16[4,1024]{1,0:T(4,128)(2,1)S(1)}, u32[]{:S(2)}) copy-start(bf16[4,1024]{1,0:T(4,128)(2,1)S(1)} %reshape.284) | copy-start | bytes 24580
  13.3 8.5 %copy-start.37 = (f32[1024]{0:T(1024)S(1)}, f32[1024]{0:T(1024)}, u32[]{:S(2)}) copy-start(f32[1024]{0:T(1024)} %param.22) | copy-start | bytes 12292
  13.3 8.5 %copy-start.38 = (f32[1024]{0:T(1024)S(1)}, f32[1024]{0:T(1024)}, u32[]{:S(2)}) copy-start(f32[1024]{0:T(1024)} %param.21) | copy-start | bytes 12292
  13.3 8.5 %copy-start.41 = (s32[2]{0:T(128)S(1)}, s32[2]{0:T(128)}, u32[]{:S(2)}) copy-start(s32[2]{0:T(128)} %param.17) | copy-start | bytes 28
  17.7 7.3 %all-to-all-start = ((f32[2,2,3072]{2,1,0:T(2,128)}), f32[2,2,3072]{2,1,0:T(2,128)S(1)}, u32[]{:S(2)}, u32[]{:S(2)}) async-start(f32[2,2,3072]{2,1,0:T(2,128)} %all_to_all.24), calls=%async_computation | async-start | bytes 98304 | tf_op jit(solution)/shard_map/all_to_all | solution.py:102
  21.0 201.1 %reduce-scatter.9.cloned.1.call-start = ((), (), s32[]{:S(2)}) async-start(), calls=%async_computation.11 | async-start | bytes 12976128 | tf_op jit(solution)/shard_map/reduce_scatter | solution.py:60
  21.3 11.1 %copy-start.32 = (f32[2,256]{1,0:T(2,128)}, f32[2,256]{1,0:T(2,128)S(1)}, u32[]{:S(2)}) copy-start(f32[2,256]{1,0:T(2,128)S(1)} %broadcast_multiply_fusion.5) | copy-start | bytes 6148
  21.7 10.7 %copy-start.34 = (f32[2,256]{1,0:T(2,128)}, f32[2,256]{1,0:T(2,128)S(1)}, u32[]{:S(2)}) copy-start(f32[2,256]{1,0:T(2,128)S(1)} %add_rsqrt_fusion.1) | copy-start | bytes 6148
  25.6 6.8 %copy-start.15 = (bf16[2,256,1024]{2,1,0:T(8,128)(2,1)}, bf16[2,256,1024]{2,1,0:T(8,128)(2,1)S(1)}, u32[]{:S(2)}) copy-start(bf16[2,256,1024]{2,1,0:T(8,128)(2,1)S(1)} %fusion.21) | copy-start | bytes 3145732
  72.7 4.3 slice-start.3
  72.7 4.3 copy-start.39
  73.1 43.7 %copy-start.2 = (f32[2,256,1024]{2,1,0:T(8,128)}, f32[2,256,1024]{2,1,0:T(8,128)S(1)}, u32[]{:S(2)}) copy-start(f32[2,256,1024]{2,1,0:T(8,128)S(1)} %get-tuple-element.31) | copy-start | bytes 6291460
  74.0 11.4 %copy-start.13 = (bf16[2,256,1024]{2,1,0:T(8,128)(2,1)}, bf16[2,256,1024]{2,1,0:T(8,128)(2,1)S(1)}, u32[]{:S(2)}) copy-start(bf16[2,256,1024]{2,1,0:T(8,128)(2,1)S(1)} %add_convert_fusion.1) | copy-start | bytes 3145732
  77.0 8.5 %copy-start.10 = (bf16[2,256,1024]{2,1,0:T(8,128)(2,1)S(1)}, bf16[2,256,1024]{2,1,0:T(8,128)(2,1)}, u32[]{:S(2)}) copy-start(bf16[2,256,1024]{2,1,0:T(8,128)(2,1)} %param.29) | copy-start | bytes 3145732
  85.5 23.7 %copy-start.11 = (bf16[512,4096]{1,0:T(8,128)(2,1)}, bf16[512,4096]{1,0:T(8,128)(2,1)S(1)}, u32[]{:S(2)}) copy-start(bf16[512,4096]{1,0:T(8,128)(2,1)S(1)} %get-tuple-element.55) | copy-start | bytes 12582916
  85.9 16.8 %copy-start.23 = (bf16[2,256,1024]{2,1,0:T(8,128)(2,1)}, bf16[2,256,1024]{2,1,0:T(8,128)(2,1)S(1)}, u32[]{:S(2)}) copy-start(bf16[2,256,1024]{2,1,0:T(8,128)(2,1)S(1)} %get-tuple-element.26) | copy-start | bytes 3145732
  102.7 6.6 %copy-start.40 = (f32[1024]{0:T(1024)S(1)}, f32[1024]{0:T(1024)}, u32[]{:S(2)}) copy-start(f32[1024]{0:T(1024)} %param.28) | copy-start | bytes 12292
  109.2 7.7 %copy-start.4 = (f32[512,1024]{1,0:T(8,128)}, f32[512,1024]{1,0:T(8,128)S(1)}, u32[]{:S(2)}) copy-start(f32[512,1024]{1,0:T(8,128)S(1)} %get-tuple-element.58) | copy-start | bytes 6291460
  133.5 14.4 %slice-start = ((s8[8388608]{0:T(1024)(128)(4,1)}), s8[4194304]{0:T(1024)(128)(4,1)S(1)}, s32[]{:S(2)}) async-start(s8[8388608]{0:T(1024)(128)(4,1)} %bitcast.188), calls=%async_computation.20 | async-start | bytes 8388608
  139.1 4.5 copy-start.18
  139.1 8.8 %slice-start.1 = ((s8[8388608]{0:T(1024)(128)(4,1)}), s8[4194304]{0:T(1024)(128)(4,1)S(1)}, s32[]{:S(2)}) async-start(s8[8388608]{0:T(1024)(128)(4,1)} %bitcast.188), calls=%async_computation.21 | async-start | bytes 8388608
  147.9 3.9 copy-start.16
  152.9 3.7 copy-start.20
  155.4 3.6 copy-start.25
  161.2 8.0 %copy-start.19 = (bf16[512,4,2,4,2,2,8]{0,6,5,4,3,2,1:T(8,128)(2,1)S(1)}, bf16[512,4,2,4,2,2,8]{0,6,5,4,3,2,1:T(8,128)(2,1)}, u32[]{:S(2)}) copy-start(bf16[512,4,2,4,2,2,8]{0,6,5,4,3,2,1:T(8,128)(2,1)} %convert_element_type.136) | copy-start | bytes 3145732
  173.9 5.8 %copy-start.21 = (bf16[1024,1024]{1,0:T(8,128)(2,1)S(1)}, bf16[1024,1024]{1,0:T(8,128)(2,1)}, u32[]{:S(2)}) copy-start(bf16[1024,1024]{1,0:T(8,128)(2,1)} %convolution_convert_fusion.1) | copy-start | bytes 6291460
  183.4 69.7 %reduce-scatter.17.cloned.1.call-start = ((), (), s32[]{:S(2)}) async-start(), calls=%async_computation.15 | async-start | bytes 25559040 | tf_op jit(solution)/shard_map/reduce_scatter | solution.py:60
  200.3 10.1 %copy-start.12 = (bf16[512,4,4,2,4,2,2,8]{0,7,6,3,2,4,5,1:T(8,128)(2,1)S(1)}, bf16[512,4,4,2,4,2,2,8]{0,7,6,3,2,4,5,1:T(8,128)(2,1)}, u32[]{:S(2)}) copy-start(bf16[512,4,4,2,4,2,2,8]{0,7,6,3,2,4,5,1:T(8,128)(2,1)} %copy.194) | copy-start | bytes 12582916
  200.3 10.1 %copy-start.24 = (bf16[2,256,1024]{2,1,0:T(8,128)(2,1)S(1)}, bf16[2,256,1024]{2,1,0:T(8,128)(2,1)}, u32[]{:S(2)}) copy-start(bf16[2,256,1024]{2,1,0:T(8,128)(2,1)} %copy-done.23) | copy-start | bytes 3145732
  222.0 82.7 %reduce-scatter.11.cloned.1.call-start = ((), (), s32[]{:S(2)}) async-start(), calls=%async_computation.12 | async-start | bytes 5406720 | tf_op jit(solution)/shard_map/reduce_scatter | solution.py:60
  222.7 165.8 %reduce-scatter.19.cloned.1.call-start = ((), (), s32[]{:S(2)}) async-start(), calls=%async_computation.16 | async-start | bytes 10649600 | tf_op jit(solution)/shard_map/reduce_scatter | solution.py:60
  253.1 135.8 %copy-start.28 = (f32[2,1024]{1,0:T(2,128)S(1)}, f32[2,1024]{1,0:T(2,128)}, u32[]{:S(2)}) copy-start(f32[2,1024]{1,0:T(2,128)} %copy-done.27) | copy-start | bytes 24580
  253.1 159.1 %reduce-scatter.13.cloned.1.call-start = ((), (), s32[]{:S(2)}) async-start(), calls=%async_computation.13 | async-start | bytes 1351680 | tf_op jit(solution)/shard_map/reduce_scatter | solution.py:60
  304.8 139.6 %reduce-scatter.21.cloned.1.call-start = ((), (), s32[]{:S(2)}) async-start(), calls=%async_computation.17 | async-start | bytes 2662400 | tf_op jit(solution)/shard_map/reduce_scatter | solution.py:60
  388.5 8.9 %copy-start.33 = (f32[2,256]{1,0:T(2,128)S(1)}, f32[2,256]{1,0:T(2,128)}, u32[]{:S(2)}) copy-start(f32[2,256]{1,0:T(2,128)} %copy-done.32) | copy-start | bytes 6148
  388.5 8.9 %copy-start.35 = (f32[2,256]{1,0:T(2,128)S(1)}, f32[2,256]{1,0:T(2,128)}, u32[]{:S(2)}) copy-start(f32[2,256]{1,0:T(2,128)} %copy-done.34) | copy-start | bytes 6148
  388.5 99.6 %reduce-scatter.15.cloned.1.call-start = ((), (), s32[]{:S(2)}) async-start(), calls=%async_computation.14 | async-start | bytes 405504 | tf_op jit(solution)/shard_map/reduce_scatter | solution.py:60
  397.4 3.4 copy-start.6
  397.4 3.7 copy-start.7
  401.1 49.9 %copy-start.30 = (bf16[4,1024]{1,0:T(4,128)(2,1)S(1)}, bf16[4,1024]{1,0:T(4,128)(2,1)}, u32[]{:S(2)}) copy-start(bf16[4,1024]{1,0:T(4,128)(2,1)} %copy-done.29) | copy-start | bytes 24580
  401.1 73.1 %copy-start.42 = (u32[128]{0:T(128)S(1)}, u32[128]{0:T(128)}, u32[]{:S(2)}) copy-start(u32[128]{0:T(128)} %constant.77) | copy-start | bytes 1540
  412.2 75.9 %reduce-scatter.23.cloned.1.call-start = ((), (), s32[]{:S(2)}) async-start(), calls=%async_computation.18 | async-start | bytes 798720 | tf_op jit(solution)/shard_map/reduce_scatter | solution.py:60
  444.4 70.5 %all-gather.4.cloned.1.call-start = ((), (), s32[]{:S(2)}) async-start(), calls=%async_computation.10 | async-start | bytes 2621440 | tf_op jit(solution)/shard_map/all_gather | solution.py:71
  451.0 36.5 %copy-start.36 = (bf16[2,1024]{1,0:T(2,128)(2,1)S(1)}, bf16[2,1024]{1,0:T(2,128)(2,1)}, u32[]{:S(2)}) copy-start(bf16[2,1024]{1,0:T(2,128)(2,1)} %param.16) | copy-start | bytes 12292
  474.1 77.8 %all-reduce.8.cloned.1.call-start = ((), (), s32[]{:S(2)}) async-start(), calls=%async_computation.19 | async-start | bytes 802816
  476.1 81.2 %copy-start.1 = (bf16[1024,1024]{1,0:T(8,128)(2,1)S(1)}, bf16[1024,1024]{1,0:T(8,128)(2,1)}, u32[]{:S(2)}) copy-start(bf16[1024,1024]{1,0:T(8,128)(2,1)} %param.23) | copy-start | bytes 6291460
  (10 other events, 16.6 us)
Sparse Core Ops, SparseCore 0:
  183.5 21.7 reduce-scatter.8
  222.1 30.9 reduce-scatter.16
  255.7 49.0 reduce-scatter.10
  307.2 81.2 reduce-scatter.18
  390.8 21.3 reduce-scatter.12
  414.5 29.8 reduce-scatter.20
  446.7 17.5 reduce-scatter.14
  466.8 18.0 reduce-scatter.22
  486.6 28.2 all-gather.3
  517.2 34.7 all-reduce.7
where the time goes:
time: 574 us; the launch traced here: 565 us
  waiting for transfers between devices  267 us (47%)
  matrix products  124 us (22%)
  local copies, waits for them, and re-layouts  79 us (14%)
  blocking collectives  40.8 us (7%)
  other arithmetic  33.3 us (6%)
  between operations  16.9 us (3%)
    reduce_scatter x8, waiting for transfers between devices, reduce_stages(): packed = lax.psum_scatter(packed, a, scatter_dimension=0, tiled=True)  205 us
    dot_general x5, matrix products, right_trans(): lax.dot_general(left, right, (((1,), (1,)), ((), ())), preferred_element_...  38.7 us
    dot_general x8, matrix products, left_trans(): lax.dot_general(left, right, (((0,), (0,)), ((), ())), preferred_element_...  32.8 us
    unnamed x11, waiting for transfers between devices  32 us
    dot_general x5, matrix products, matmul(): return jnp.dot(left, right, preferred_element_type=jnp.float32)  27.9 us
    all_gather x1, waiting for transfers between devices, gather_dp(): values = lax.all_gather(values, a, axis=0, tiled=True)  26.7 us
    all_gather x3, blocking collectives, gather_dp(): values = lax.all_gather(values, a, axis=0, tiled=True)  23.1 us
    unnamed x108, local copies, waits for them, and re-layouts  13.5 us
  transfers between devices with their start and end apart: 11, of which 8 were waited for; matrix products, arithmetic and copies ran while one was open for 12% of the time, Pallas kernels for 0%

commit v1 on v0

--- a/solution.py
+++ b/solution.py
@@ -55,10 +55,19 @@
     return jnp.transpose(values, order).reshape(*lead, -1)
 
 
-def reduce_stages(packed):
-    for a in STAGES:
+def reduce_stages(packed, stages):
+    for a in stages:
         packed = lax.psum_scatter(packed, a, scatter_dimension=0, tiled=True)
-    return packed.astype(jnp.float32)
+    return packed
+
+
+def reduce_rest(packed, axes):
+    count = 1
+    for a in axes:
+        count *= lax.axis_size(a)
+    chunks = packed.reshape(count, packed.shape[0] // count, packed.shape[1])
+    chunks = lax.all_to_all(chunks, axes, 0, 0, tiled=False)
+    return jnp.sum(chunks.astype(jnp.float32), axis=0)
 
 
 def bias_columns(columns, rows):
@@ -67,9 +76,11 @@
 
 
 def gather_dp(values):
-    for a in ("c", "x", "zh", "y"):
-        values = lax.all_gather(values, a, axis=0, tiled=True)
-    return values
+    count = 1
+    for a in DP:
+        count *= lax.axis_size(a)
+    copies = jnp.broadcast_to(values[None], (count,) + values.shape)
+    return lax.all_to_all(copies, DP, 0, 0, tiled=False).reshape(-1, values.shape[1])
 
 
 def per_device(
@@ -179,7 +190,8 @@
             + contract_parts
             + [bias_columns([contract_bias_grad] + [expand_bias_grad[q] for q in range(split)], width)],
             axis=1,
-        )
+        ),
+        STAGES[:2],
     )
     grad_mod_b = right_trans(grad_exp_b, expand_weight).reshape(images, rows, width)
     grad_shift_b = jnp.sum(grad_mod_b, axis=1)
@@ -234,7 +246,8 @@
                 bias_columns([query_bias_grad, value_bias_grad, output_bias_grad], width),
             ],
             axis=1,
-        )
+        ),
+        STAGES[:2],
     )
     grad_mod_a = right_trans(grad_proj_b, input_weight).reshape(images, rows, width)
     grad_shift_a = jnp.sum(grad_mod_a, axis=1)
@@ -258,6 +271,9 @@
     modulation_weight_grad = left_trans(silu_rows, mod_all)
     bias_all = jnp.sum(mod_all.astype(jnp.float32), axis=0).reshape(-1, width)
     modulation_bias_grad = lax.dynamic_slice_in_dim(bias_all, dp_index * row_block, row_block, axis=1)
+    rest = reduce_rest(jnp.concatenate([chain_a, chain_b], axis=1), STAGES[2:])
+    chain_a = rest[:, : chain_a.shape[1]]
+    chain_b = rest[:, chain_a.shape[1] :]
     three = input_weight.shape[1]
     fw = expand_weight.shape[1]
     input_weight_grad = chain_b[:, :three]

time: 574 us -> 494 us (0.86)
  waiting for transfers between devices: 267 us -> 155 us
  starting transfers between devices: 3.96 us -> 21.3 us
  blocking collectives: 40.8 us -> 47.7 us
    reduce_scatter x8 -> x4, waiting for transfers between devices: 205 us -> 151 us  [reduce_stages(): packed = lax.psum_scatter(packed, a, scatter_dimension=0, tiled=True)]
    unnamed x11 -> x4, waiting for transfers between devices: 32 us -> 0.7 us
    unnamed x1, blocking collectives: 6.73 us -> 36.8 us
    all_gather x1 -> x0, waiting for transfers between devices: 26.7 us -> none  [gather_dp(): values = lax.all_gather(values, a, axis=0, tiled=True)]
    all_gather x3 -> x0, blocking collectives: 23.1 us -> none  [gather_dp(): values = lax.all_gather(values, a, axis=0, tiled=True)]
    all_to_all x0 -> x2, starting transfers between devices: none -> 17.6 us  [the longest x1 10.2 us: gather_dp(): lax.all_to_all(copies, DP, 0, 0, tiled=False).reshape(-1, values.shape[1])]
    unnamed x108 -> x111, local copies, waits for them, and re-layouts: 13.5 us -> 14.6 us
  transfers between devices with their start and end apart: 11 -> 7, of which waited for: 8 -> 4; matrix products, arithmetic and copies ran while one was open for 12% -> 15% of each run, Pallas kernels for 0% -> 0%
where the time goes in v1:
time: 494 us; the launch traced here: 486 us
  waiting for transfers between devices  155 us (31%)
  matrix products  124 us (25%)
  local copies, waits for them, and re-layouts  84.1 us (17%)
  blocking collectives  47.7 us (10%)
  other arithmetic  37.9 us (8%)
  starting transfers between devices  21.3 us (4%)
  between operations  15.8 us (3%)
    reduce_scatter x4, waiting for transfers between devices, reduce_stages(): packed = lax.psum_scatter(packed, a, scatter_dimension=0, tiled=True)  151 us
    dot_general x5, matrix products, right_trans(): lax.dot_general(left, right, (((1,), (1,)), ((), ())), preferred_element_...  38.6 us
    unnamed x1, blocking collectives  36.8 us
    dot_general x8, matrix products, left_trans(): lax.dot_general(left, right, (((0,), (0,)), ((), ())), preferred_element_...  32.8 us
    dot_general x5, matrix products, matmul(): return jnp.dot(left, right, preferred_element_type=jnp.float32)  27.9 us
    unnamed x111, local copies, waits for them, and re-layouts  14.6 us
    all_to_all x1, starting transfers between devices, gather_dp(): lax.all_to_all(copies, DP, 0, 0, tiled=False).reshape(-1, values.shape[1])  10.2 us
  transfers between devices with their start and end apart: 7, of which 4 were waited for; matrix products, arithmetic and copies ran while one was open for 15% of the time, Pallas kernels for 0%

profile of v1, /device:TPU:24, one launch (start us, length us, event | category | flops | bytes accessed | tf_op | source)
XLA Modules:
  0.0 485.6 jit_solution(3683518201547290799)
XLA Ops:
  8.1 4.3 all-gather
  13.2 3.8 convolution_add_fusion
  17.6 3.3 all-to-all-start
  21.7 3.2 all-to-all-done
  25.6 6.8 %add_convert_fusion = bf16[512,3072]{1,0:T(8,128)(2,1)S(1)} fusion(bf16[512,1024]{1,0:T(8,128)(2,1)S(1)} %bitcast.196, bf16[1024,3072]{1,0:T(8,128)(2,1)} %param.20, f32[3072]{0:T(1024)S(1)} %pad_maximum_fusion.1), kind=kOutput, calls=%fused_computation.21 | convolution fusion | flops 3224371200 | bytes 10498048 | tf_op jit(solution)/shard_map/dot_general | solution.py:20
  34.1 4.0 reshape.295
  38.1 3.5 copy.216
  41.7 4.0 reshape.296
  45.7 3.6 copy.214
  49.3 4.0 reshape.297
  53.3 3.7 copy.215
  57.0 7.7 %fusion.72 = (f32[2,16,256]{2,1,0:T(8,128)S(1)}, f32[2,16,256,256]{2,3,1,0:T(8,128)}) fusion(bf16[2,256,16,64]{1,3,2,0:T(8,128)(2,1)} %copy.214, bf16[2,256,16,64]{1,3,2,0:T(8,128)(2,1)} %copy.215), kind=kOutput, calls=%fused_computation.147 | convolution fusion | flops 274727168 | bytes 10518528 | tf_op jit(solution)/shard_map/sub | solution.py:135
  64.7 4.6 fusion.46
  74.5 2.5 slice-done.3
  76.9 8.5 %multiply_convert_fusion.1 = (bf16[512,4096]{1,0:T(8,128)(2,1)S(1)}, f32[512,4096]{1,0:T(8,128)}) fusion(f32[4096]{0:T(1024)S(1)} %copy-done.41, bf16[512,1024]{1,0:T(8,128)(2,1)S(1)} %bitcast.195, bf16[1024,4096]{1,0:T(8,128)(2,1)S(1)} %bitcast.227), kind=kOutput, calls=%fused_computation.16 | convolution fusion | flops 4315938816 | bytes 22036480 | tf_op jit(solution)/shard_map/dot_general | solution.py:20
  85.8 16.7 %fusion.73 = (bf16[4096]{0:T(1024)(128)(2,1)S(1)}, bf16[512,4096]{1,0:T(8,128)(2,1)}) fusion(f32[512,4096]{1,0:T(8,128)} %get-tuple-element.55, f32[4096]{0:T(1024)S(1)} %copy-done.41, bf16[512,1024]{1,0:T(8,128)(2,1)S(1)} %bitcast.206, bf16[4096,1024]{1,0:T(8,128)(2,1)} %param.27), kind=kOutput, calls=%fused_computation.148 | convolution fusion | flops 4339003392 | bytes 22044672 | tf_op jit(solution)/shard_map/dot_general | solution.py:30
  102.6 6.5 %fusion.29 = (f32[512]{0:T(512)S(1)}, f32[512,1024]{1,0:T(8,128)S(1)}) fusion(f32[2,1024]{1,0:T(2,128)S(1)} %get-tuple-element.45, bf16[512,4096]{1,0:T(8,128)(2,1)} %get-tuple-element.63, bf16[1024,4096]{1,0:T(8,128)(2,1)S(1)} %bitcast.227), kind=kOutput, calls=%fused_computation.49 | convolution fusion | flops 4296015360 | bytes 14690304 | tf_op jit(solution)/shard_map/dot_general | solution.py:30
  109.2 7.6 %convolution_add_fusion.2 = f32[512,1024]{1,0:T(8,128)S(1)} fusion(bf16[512,4096]{1,0:T(8,128)(2,1)S(1)} %get-tuple-element.54, bf16[4096,1024]{1,0:T(8,128)(2,1)} %param.27, f32[1024]{0:T(1024)S(1)} %copy-done.42), kind=kOutput, calls=%fused_computation.76 | convolution fusion | flops 4295491584 | bytes 14684160 | tf_op jit(solution)/shard_map/dot_general | solution.py:20
  116.8 2.8 fusion.30
  119.7 4.9 %fusion.66 = (bf16[1024]{0:T(1024)(128)(2,1)S(1)}, bf16[2,256,1024]{2,1,0:T(8,128)(2,1)S(1)}, f32[2,256,1024]{2,1,0:T(8,128)}) fusion(f32[2,1024]{1,0:T(2,128)S(1)} %get-tuple-element.48, f32[2,256]{1,0:T(2,128)S(1)} %broadcast_multiply_fusion.3, f32[2,256,1024]{2,1,0:T(8,128)} %copy-done.2, f32[2,256]{1,0:T(2,128)S(1)} %broadcast_multiply_fusion.4, ...), kind=kLoop, calls=%fused_computation.141 | loop fusion | flops 6814720 | bytes 8415240 | tf_op jit(solution)/shard_map/reduce_sum | solution.py:206
  127.8 3.1 reshape.298
  130.9 2.5 copy.220
  133.4 5.6 %multiply_reduce_fusion = (f32[2,16,256]{2,1,0:T(8,128)S(1)}, f32[2,16,256,256]{2,3,1,0:T(8,128)S(1)}) fusion(f32[2,16,256,256]{2,3,1,0:T(8,128)} %get-tuple-element.53, f32[2,16,256]{2,1,0:T(8,128)S(1)} %get-tuple-element.52, bf16[2,256,16,64]{1,3,2,0:T(8,128)(2,1)} %copy.220, bf16[2,256,16,64]{1,3,2,0:T(8,128)(2,1)} %copy.216), kind=kOutput, calls=%fused_computation.15 | convolution fusion | flops 274718720 | bytes 18939904 | tf_op jit(solution)/shard_map/bqhe,bkhe->bhqk/dot_general | solution.py:213
  139.0 4.5 multiply_convert_fusion
  167.1 3.8 convolution_convert_fusion.1
  171.6 5.7 %convolution_convert_fusion = bf16[1024,3072]{1,0:T(8,128)(2,1)S(1)} fusion(bf16[512,1024]{0,1:T(8,128)(2,1)S(1)} %bitcast.213, bf16[512,3072]{0,1:T(8,128)(2,1)} %constant_dynamic-update-slice_fusion), kind=kOutput, calls=%fused_computation.22 | convolution fusion | flops 3224371200 | bytes 10485760 | tf_op jit(solution)/shard_map/dot_general | solution.py:24
  177.4 3.7 fusion.2
  183.5 6.5 %copy.235 = bf16[512,4096]{0,1:T(8,128)(2,1)} copy(bf16[512,4096]{1,0:T(8,128)(2,1)} %copy-done.13) | data formatting | bytes 8388608 | tf_op jit(solution)/shard_map/convert_element_type | solution.py:148
  190.8 6.0 %copy.236 = bf16[512,4,4,2,4,2,2,8]{0,7,6,3,2,4,5,1:T(8,128)(2,1)} copy(bf16[512,4,4,2,4,2,2,8]{0,7,1,6,5,4,3,2:T(8,128)(2,1)} %bitcast.186) | data formatting | bytes 8388608 | tf_op jit(solution)/shard_map/reshape;reshape | solution.py:52
  198.1 10.0 %convert_dynamic-update-slice_fusion = bf16[1024,8320]{1,0:T(8,128)(2,1)} fusion(bf16[512,1024]{0,1:T(8,128)(2,1)S(1)} %bitcast.211, bf16[512,4096]{1,0:T(8,128)(2,1)} %get-tuple-element.63), kind=kOutput, calls=%fused_computation.13 | convolution fusion | flops 4299161600 | bytes 13631488 | tf_op jit(solution)/shard_map/dot_general | solution.py:24
  208.2 2.7 convert_dynamic-update-slice_fusion.4
  210.8 2.7 convert_dynamic-update-slice_fusion.3
  213.5 2.7 convert_dynamic-update-slice_fusion.2
  216.2 2.7 convert_dynamic-update-slice_fusion.1
  220.8 30.0 %reduce-scatter.5.cloned.1.call-done = bf16[512,8320]{1,0:T(8,128)(2,1)} async-done(((bf16[1024,8320]{1,0:T(8,128)(2,1)}), bf16[512,8320]{1,0:T(8,128)(2,1)}) %reduce-scatter.5.cloned.1.call-update) | async-done | bytes 8519696 | tf_op jit(solution)/shard_map/reduce_scatter | solution.py:60
  251.5 8.6 %fusion.28 = (f32[512]{0:T(512)S(1)}, f32[512,1024]{1,0:T(8,128)}) fusion(f32[2,1024]{1,0:T(2,128)S(1)} %copy-done.30, bf16[512,3072]{0,1:T(8,128)(2,1)} %constant_dynamic-update-slice_fusion, bf16[1024,3072]{1,0:T(8,128)(2,1)} %param.20), kind=kOutput, calls=%fused_computation.46 | convolution fusion | flops 3222273536 | bytes 11544576 | tf_op jit(solution)/shard_map/dot_general | solution.py:30
  260.1 3.2 fusion.26
  263.7 4.1 multiply_reduce_fusion.3
  267.8 6.6 %all_to_all.42 = bf16[2,2,3072]{2,0,1:T(2,128)(2,1)S(1)} all-to-all(bf16[2,2,3072]{2,0,1:T(2,128)(2,1)S(1)} %bitcast.225), channel_id=1, replica_groups=mesh['y'=4,'zh'=2,'x'=4,'c'=2,'zl'=2] {'zl'}, dimensions={1} | all-to-all | bytes 49152 | tf_op jit(solution)/shard_map/all_to_all | solution.py:260
  276.8 10.2 %all-to-all-start.2 = ((bf16[64,4,4096]{2,1,0:T(4,128)(2,1)}), bf16[64,4,4096]{2,1,0:T(4,128)(2,1)S(1)}, u32[]{:S(2)}, u32[]{:S(2)}) async-start(bf16[64,4,4096]{2,1,0:T(4,128)(2,1)} %broadcast_in_dim.5), calls=%async_computation.2 | async-start | bytes 4194304 | tf_op jit(solution)/shard_map/all_to_all | solution.py:83
  287.1 36.1 %reduce-scatter.11.cloned.1.call-done = bf16[128,4224]{1,0:T(8,128)(2,1)} async-done(((bf16[512,4224]{1,0:T(8,128)(2,1)}), bf16[128,4224]{1,0:T(8,128)(2,1)}) %reduce-scatter.11.cloned.1.call-update) | async-done | bytes 1081360 | tf_op jit(solution)/shard_map/reduce_scatter | solution.py:60
  323.2 84.7 %reduce-scatter.7.cloned.1.call-done = bf16[128,8320]{1,0:T(8,128)(2,1)} async-done(((bf16[512,8320]{1,0:T(8,128)(2,1)}), bf16[128,8320]{1,0:T(8,128)(2,1)}) %reduce-scatter.7.cloned.1.call-update) | async-done | bytes 2129936 | tf_op jit(solution)/shard_map/reduce_scatter | solution.py:60
  407.9 3.8 maximum_bitcast_fusion
  413.1 7.4 %all-to-all-start.3 = ((bf16[16,8,12544]{2,1,0:T(8,128)(2,1)}), bf16[16,8,12544]{2,1,0:T(8,128)(2,1)}, u32[]{:S(2)}, u32[]{:S(2)}) async-start(bf16[16,8,12544]{2,1,0:T(8,128)(2,1)} %maximum_bitcast_fusion), calls=%async_computation.7 | async-start | bytes 6422528 | tf_op jit(solution)/shard_map/all_to_all | solution.py:69
  421.8 4.5 fusion.74
  426.3 36.8 %all-reduce.2 = f32[4,1024]{1,0:T(4,128)S(1)} all-reduce(f32[4,1024]{1,0:T(4,128)S(1)} %fusion.74), channel_id=2, replica_groups=mesh['y'=4,'zh'=2,'x'=4,'c'=2,'zl'=2] {'zl'}, use_global_device_ids=true, to_apply=%region_17.18.clone | all-reduce | flops 4096 | bytes 32768
  463.7 2.5 reshape.274
  470.2 2.5 fusion.41
  (213 shorter events, 60.4 us)
Async XLA Ops:
  7.2 64.2 %copy-start = (bf16[1024,1024]{1,0:T(8,128)(2,1)S(1)}, bf16[1024,1024]{1,0:T(8,128)(2,1)}, u32[]{:S(2)}) copy-start(bf16[1024,1024]{1,0:T(8,128)(2,1)} %param.23) | copy-start | bytes 6291460
  12.4 5.2 %copy-start.31 = (bf16[4,1024]{1,0:T(4,128)(2,1)}, bf16[4,1024]{1,0:T(4,128)(2,1)S(1)}, u32[]{:S(2)}) copy-start(bf16[4,1024]{1,0:T(4,128)(2,1)S(1)} %reshape.293) | copy-start | bytes 24580
  13.1 7.8 %copy-start.3 = (bf16[2,256,1024]{2,1,0:T(8,128)(2,1)S(1)}, bf16[2,256,1024]{2,1,0:T(8,128)(2,1)}, u32[]{:S(2)}) copy-start(bf16[2,256,1024]{2,1,0:T(8,128)(2,1)} %param.15) | copy-start | bytes 3145732
  13.1 8.5 %copy-start.39 = (f32[1024]{0:T(1024)S(1)}, f32[1024]{0:T(1024)}, u32[]{:S(2)}) copy-start(f32[1024]{0:T(1024)} %param.22) | copy-start | bytes 12292
  13.2 8.5 %copy-start.40 = (f32[1024]{0:T(1024)S(1)}, f32[1024]{0:T(1024)}, u32[]{:S(2)}) copy-start(f32[1024]{0:T(1024)} %param.21) | copy-start | bytes 12292
  13.2 8.5 %copy-start.43 = (s32[2]{0:T(128)S(1)}, s32[2]{0:T(128)}, u32[]{:S(2)}) copy-start(s32[2]{0:T(128)} %param.17) | copy-start | bytes 28
  17.6 7.3 %all-to-all-start = ((f32[2,2,3072]{2,1,0:T(2,128)}), f32[2,2,3072]{2,1,0:T(2,128)S(1)}, u32[]{:S(2)}, u32[]{:S(2)}) async-start(f32[2,2,3072]{2,1,0:T(2,128)} %all_to_all.30), calls=%async_computation | async-start | bytes 98304 | tf_op jit(solution)/shard_map/all_to_all | solution.py:113
  20.9 198.8 %reduce-scatter.9.cloned.1.call-start = ((), (), s32[]{:S(2)}) async-start(), calls=%async_computation.10 | async-start | bytes 12976128 | tf_op jit(solution)/shard_map/reduce_scatter | solution.py:60
  21.2 11.1 %copy-start.34 = (f32[2,256]{1,0:T(2,128)}, f32[2,256]{1,0:T(2,128)S(1)}, u32[]{:S(2)}) copy-start(f32[2,256]{1,0:T(2,128)S(1)} %broadcast_multiply_fusion.5) | copy-start | bytes 6148
  21.6 10.7 %copy-start.36 = (f32[2,256]{1,0:T(2,128)}, f32[2,256]{1,0:T(2,128)S(1)}, u32[]{:S(2)}) copy-start(f32[2,256]{1,0:T(2,128)S(1)} %add_rsqrt_fusion.1) | copy-start | bytes 6148
  25.6 6.8 %copy-start.17 = (bf16[2,256,1024]{2,1,0:T(8,128)(2,1)}, bf16[2,256,1024]{2,1,0:T(8,128)(2,1)S(1)}, u32[]{:S(2)}) copy-start(bf16[2,256,1024]{2,1,0:T(8,128)(2,1)S(1)} %fusion.21) | copy-start | bytes 3145732
  69.3 2.1 copy-start.33
  71.4 3.1 slice-start.2
  72.6 4.3 slice-start.3
  73.0 43.7 %copy-start.2 = (f32[2,256,1024]{2,1,0:T(8,128)}, f32[2,256,1024]{2,1,0:T(8,128)S(1)}, u32[]{:S(2)}) copy-start(f32[2,256,1024]{2,1,0:T(8,128)S(1)} %get-tuple-element.30) | copy-start | bytes 6291460
  73.0 3.9 copy-start.41
  74.4 11.0 %copy-start.15 = (bf16[2,256,1024]{2,1,0:T(8,128)(2,1)}, bf16[2,256,1024]{2,1,0:T(8,128)(2,1)S(1)}, u32[]{:S(2)}) copy-start(bf16[2,256,1024]{2,1,0:T(8,128)(2,1)S(1)} %add_convert_fusion.1) | copy-start | bytes 3145732
  76.9 8.5 %copy-start.11 = (bf16[2,256,1024]{2,1,0:T(8,128)(2,1)S(1)}, bf16[2,256,1024]{2,1,0:T(8,128)(2,1)}, u32[]{:S(2)}) copy-start(bf16[2,256,1024]{2,1,0:T(8,128)(2,1)} %param.29) | copy-start | bytes 3145732
  85.4 23.7 %copy-start.13 = (bf16[512,4096]{1,0:T(8,128)(2,1)}, bf16[512,4096]{1,0:T(8,128)(2,1)S(1)}, u32[]{:S(2)}) copy-start(bf16[512,4096]{1,0:T(8,128)(2,1)S(1)} %get-tuple-element.54) | copy-start | bytes 12582916
  85.8 16.8 %copy-start.25 = (bf16[2,256,1024]{2,1,0:T(8,128)(2,1)}, bf16[2,256,1024]{2,1,0:T(8,128)(2,1)S(1)}, u32[]{:S(2)}) copy-start(bf16[2,256,1024]{2,1,0:T(8,128)(2,1)S(1)} %get-tuple-element.25) | copy-start | bytes 3145732
  102.6 6.6 %copy-start.42 = (f32[1024]{0:T(1024)S(1)}, f32[1024]{0:T(1024)}, u32[]{:S(2)}) copy-start(f32[1024]{0:T(1024)} %param.28) | copy-start | bytes 12292
  109.1 7.7 %copy-start.4 = (f32[512,1024]{1,0:T(8,128)}, f32[512,1024]{1,0:T(8,128)S(1)}, u32[]{:S(2)}) copy-start(f32[512,1024]{1,0:T(8,128)S(1)} %get-tuple-element.57) | copy-start | bytes 6291460
  133.4 14.4 %slice-start = ((s8[8388608]{0:T(1024)(128)(4,1)}), s8[4194304]{0:T(1024)(128)(4,1)S(1)}, s32[]{:S(2)}) async-start(s8[8388608]{0:T(1024)(128)(4,1)} %bitcast.188), calls=%async_computation.12 | async-start | bytes 8388608
  139.0 4.5 copy-start.20
  139.0 8.8 %slice-start.1 = ((s8[8388608]{0:T(1024)(128)(4,1)}), s8[4194304]{0:T(1024)(128)(4,1)S(1)}, s32[]{:S(2)}) async-start(s8[8388608]{0:T(1024)(128)(4,1)} %bitcast.188), calls=%async_computation.13 | async-start | bytes 8388608
  143.5 1.8 copy-start.19
  145.3 2.5 copy-start.24
  147.8 2.5 copy-start.10
  147.8 3.9 copy-start.18
  152.9 3.7 copy-start.22
  155.5 2.4 copy-start.27
  161.5 5.4 %copy-start.21 = (bf16[512,4,2,4,2,2,8]{0,6,5,4,3,2,1:T(8,128)(2,1)S(1)}, bf16[512,4,2,4,2,2,8]{0,6,5,4,3,2,1:T(8,128)(2,1)}, u32[]{:S(2)}) copy-start(bf16[512,4,2,4,2,2,8]{0,6,5,4,3,2,1:T(8,128)(2,1)} %convert_element_type.140) | copy-start | bytes 3145732
  171.6 5.8 %copy-start.23 = (bf16[1024,1024]{1,0:T(8,128)(2,1)S(1)}, bf16[1024,1024]{1,0:T(8,128)(2,1)}, u32[]{:S(2)}) copy-start(bf16[1024,1024]{1,0:T(8,128)(2,1)} %convolution_convert_fusion.1) | copy-start | bytes 6291460
  181.2 69.6 %reduce-scatter.5.cloned.1.call-start = ((), (), s32[]{:S(2)}) async-start(), calls=%async_computation.8 | async-start | bytes 25559040 | tf_op jit(solution)/shard_map/reduce_scatter | solution.py:60
  198.1 10.1 %copy-start.14 = (bf16[512,4,4,2,4,2,2,8]{0,7,6,3,2,4,5,1:T(8,128)(2,1)S(1)}, bf16[512,4,4,2,4,2,2,8]{0,7,6,3,2,4,5,1:T(8,128)(2,1)}, u32[]{:S(2)}) copy-start(bf16[512,4,4,2,4,2,2,8]{0,7,6,3,2,4,5,1:T(8,128)(2,1)} %copy.236) | copy-start | bytes 12582916
  198.1 10.1 %copy-start.26 = (bf16[2,256,1024]{2,1,0:T(8,128)(2,1)S(1)}, bf16[2,256,1024]{2,1,0:T(8,128)(2,1)}, u32[]{:S(2)}) copy-start(bf16[2,256,1024]{2,1,0:T(8,128)(2,1)} %copy-done.25) | copy-start | bytes 3145732
  219.7 103.5 %reduce-scatter.11.cloned.1.call-start = ((), (), s32[]{:S(2)}) async-start(), calls=%async_computation.11 | async-start | bytes 5406720 | tf_op jit(solution)/shard_map/reduce_scatter | solution.py:60
  220.4 187.5 %reduce-scatter.7.cloned.1.call-start = ((), (), s32[]{:S(2)}) async-start(), calls=%async_computation.9 | async-start | bytes 10649600 | tf_op jit(solution)/shard_map/reduce_scatter | solution.py:60
  251.5 8.6 %copy-start.35 = (f32[2,256]{1,0:T(2,128)S(1)}, f32[2,256]{1,0:T(2,128)}, u32[]{:S(2)}) copy-start(f32[2,256]{1,0:T(2,128)} %copy-done.34) | copy-start | bytes 6148
  251.5 8.6 %copy-start.37 = (f32[2,256]{1,0:T(2,128)S(1)}, f32[2,256]{1,0:T(2,128)}, u32[]{:S(2)}) copy-start(f32[2,256]{1,0:T(2,128)} %copy-done.36) | copy-start | bytes 6148
  260.1 3.3 copy-start.6
  260.1 3.5 copy-start.7
  263.7 10.8 %copy-start.32 = (bf16[4,1024]{1,0:T(4,128)(2,1)S(1)}, bf16[4,1024]{1,0:T(4,128)(2,1)}, u32[]{:S(2)}) copy-start(bf16[4,1024]{1,0:T(4,128)(2,1)} %copy-done.31) | copy-start | bytes 24580
  276.8 134.9 %all-to-all-start.2 = ((bf16[64,4,4096]{2,1,0:T(4,128)(2,1)}), bf16[64,4,4096]{2,1,0:T(4,128)(2,1)S(1)}, u32[]{:S(2)}, u32[]{:S(2)}) async-start(bf16[64,4,4096]{2,1,0:T(4,128)(2,1)} %broadcast_in_dim.5), calls=%async_computation.2 | async-start | bytes 4194304 | tf_op jit(solution)/shard_map/all_to_all | solution.py:83
  411.8 8.8 %copy-start.44 = (u32[128]{0:T(128)S(1)}, u32[128]{0:T(128)}, u32[]{:S(2)}) copy-start(u32[128]{0:T(128)} %constant.77) | copy-start | bytes 1540
  413.1 59.6 %all-to-all-start.3 = ((bf16[16,8,12544]{2,1,0:T(8,128)(2,1)}), bf16[16,8,12544]{2,1,0:T(8,128)(2,1)}, u32[]{:S(2)}, u32[]{:S(2)}) async-start(bf16[16,8,12544]{2,1,0:T(8,128)(2,1)} %maximum_bitcast_fusion), calls=%async_computation.7 | async-start | bytes 6422528 | tf_op jit(solution)/shard_map/all_to_all | solution.py:69
  420.5 42.6 %copy-start.38 = (bf16[2,1024]{1,0:T(2,128)(2,1)S(1)}, bf16[2,1024]{1,0:T(2,128)(2,1)}, u32[]{:S(2)}) copy-start(bf16[2,1024]{1,0:T(2,128)(2,1)} %param.16) | copy-start | bytes 12292
  467.7 10.9 %copy-start.1 = (bf16[1024,1024]{1,0:T(8,128)(2,1)S(1)}, bf16[1024,1024]{1,0:T(8,128)(2,1)}, u32[]{:S(2)}) copy-start(bf16[1024,1024]{1,0:T(8,128)(2,1)} %param.23) | copy-start | bytes 6291460
  (8 other events, 8.6 us)
Sparse Core Ops, SparseCore 0:
  181.3 21.8 reduce-scatter.8
  219.8 30.9 reduce-scatter.4
  253.4 69.7 reduce-scatter.10
  325.7 82.2 reduce-scatter.6
